TPU v7x, 512 devices: a whole 4x4x16 slice. The times are simulated.
512 devices in a mesh: layer: 128 (over z, x, core), tile: 4 (over y).
Axes of the slice: x: 4, y: 4, z: 16, core: 2. Of those that a mesh axis runs over, the one named last changes fastest.
Arguments:
- sources: float32 [128, 2, 2, 32, 8192], P('layer', None, None, None, 'tile'), may hold values from -6 to 6
- green: float32 [128, 80, 2, 128, 128], P('layer', 'tile'), may hold values from -0.25 to 0.25
- rowcol: int32 [128, 80, 2], P('layer', 'tile'), may hold values from 0 to 63, as said below
- counts: int32 [128, 16], P('layer', 'tile'), may hold values from 1 to 5, as said below
Outputs:
- traces: float32 [128, 2, 2, 32, 8192], P('layer', None, None, None, 'tile')
Inputs may be any that keep to these rules, and one draw needn't show every extreme that they name: `rowcol`: the row tile of a slot of tile device t lies in t * 16 to (t + 1) * 16 - 1; its column tile differs from its row tile by at most 4. Kind 0 has 2 or more live slots; the four counts of one tile device sum to at most 10; in every layer some tile device has 5 live slots of kind 0 and 10 live slots in all.
All inputs are finite; a program needn't handle non-finite values.
Results may differ from a plain program's by a relative error of at most 0.0003.
Values sent between devices are 32-bit elements; how exact they have to be, the bound alone decides.
A program may use at most 64 MiB of HBM per device.

v0:
```python
import jax
import jax.numpy as jnp
from jax import lax
from jax.sharding import PartitionSpec as P

TILE = 128
CAP = 5
BAND = 4
TICKS = 6


def from_behind(block, axis, distance):
    devices = range(lax.axis_size(axis))
    route = [(i - distance, i) for i in devices if i - distance in devices]
    return lax.ppermute(block, axis, route)


def padded(cells, sides, width):
    for axis, dim in sides:
        count = lax.axis_size(axis)
        ends = count - 1
        head = lax.slice_in_dim(cells, 0, width, axis=dim)
        tail = lax.slice_in_dim(cells, cells.shape[dim] - width, cells.shape[dim], axis=dim)
        cells = jnp.concatenate(
            [
                lax.ppermute(tail, axis, [(i, (i + 1) % count) for i in range(ends)]),
                cells,
                lax.ppermute(head, axis, [((i + 1) % count, i) for i in range(ends)]),
            ],
            axis=dim,
        )
    return cells


def complex_term(picked, blocks, pattern):
    prod = jnp.einsum(pattern, picked, blocks, precision=lax.Precision.HIGHEST)
    return jnp.stack([prod[0, 0] - prod[1, 1], prod[0, 1] + prod[1, 0]])


def place_terms(terms, target, live, tiles_dev):
    onehot = (
        (target[:, None] == jnp.arange(2 * tiles_dev, dtype=jnp.int32)[None, :]) & live[:, None]
    ).astype(jnp.float32)
    onehot = onehot.reshape(target.shape[0], 2, tiles_dev)
    return jnp.einsum("csni,ngr->gcsri", terms, onehot, precision=lax.Precision.HIGHEST)


def padded_update(tiled, blocks, row_local, col_local, live_counts, tiles_dev):
    picks = []
    for kind_index in range(4):
        anchor = 1 if kind_index in (1, 2) else 0
        columns = col_local[kind_index * CAP : (kind_index + 1) * CAP]
        picks.append(jnp.take(tiled[anchor], columns, axis=2))
    picked = jnp.concatenate(picks, axis=2)
    terms = complex_term(picked, blocks, "csnj,ndij->cdsni")
    slot = jnp.arange(4 * CAP, dtype=jnp.int32)
    group = slot // CAP
    live = slot % CAP < live_counts[group]
    target = jnp.where(group < 2, 0, 1) * tiles_dev + row_local
    return place_terms(terms, target, live, tiles_dev)


def body(sources, green, rowcol, counts):
    width = sources.shape[-1]
    shots = sources.shape[3]
    tiles_dev = width // TILE
    place = lax.axis_index("tile")
    blocks = green[0]
    pairs = rowcol[0]
    live_counts = counts[0]
    row_local = pairs[:, 0] - place * tiles_dev
    col_local = pairs[:, 1] - place * tiles_dev + BAND
    local_sources = sources[0]
    waves = local_sources
    for sweep in range(TICKS - 1):
        prev_down = from_behind(waves[0], "layer", 1)
        next_up = from_behind(waves[1], "layer", -1)
        incoming = jnp.stack([prev_down, next_up])
        widened = padded(incoming, (("tile", 3),), BAND * TILE)
        tiled = widened.reshape(2, 2, shots, tiles_dev + 2 * BAND, TILE)
        update = padded_update(tiled, blocks, row_local, col_local, live_counts, tiles_dev)
        waves = local_sources + update.reshape(2, 2, shots, width)
    return waves[None]


def solution(mesh):
    return jax.shard_map(
        body,
        mesh=mesh,
        in_specs=(
            P("layer", None, None, None, "tile"),
            P("layer", "tile", None, None, None),
            P("layer", "tile", None),
            P("layer", "tile"),
        ),
        out_specs=P("layer", None, None, None, "tile"),
        check_vma=False,
    )
```

profile of v0, /device:TPU:103, one launch (start us, length us, event | category | flops | bytes accessed | tf_op | source)
XLA Modules:
  0.0 249.9 jit_solution(13530782876541986595)
XLA Ops:
  2.5 5.2 %collective-permute-start = (f32[2,32,2048]{2,1,0:T(8,128)}, f32[2,32,2048]{2,1,0:T(8,128)S(1)}, u32[]{:S(2)}, u32[]{:S(2)}) collective-permute-start(f32[2,32,2048]{2,1,0:T(8,128)} %get-tuple-element.42), channel_id=1, source_target_pairs={{0,4},{4,8},{8,12},{12,16},{16,20},{20,24},{24,28},{28,32},{32,36}... | collective-permute-start | bytes 1572872 | tf_op jit(solution)/shard_map/ppermute | solution.py:15
  10.4 3.7 %collective-permute-done = f32[2,32,2048]{2,1,0:T(8,128)S(1)} collective-permute-done((f32[2,32,2048]{2,1,0:T(8,128)}, f32[2,32,2048]{2,1,0:T(8,128)S(1)}, u32[]{:S(2)}, u32[]{:S(2)}) %collective-permute-start) | collective-permute-done | bytes 524320 | tf_op jit(solution)/shard_map/ppermute | solution.py:15
  14.1 7.7 %collective-permute-done.1 = f32[2,32,2048]{2,1,0:T(8,128)} collective-permute-done((f32[2,32,2048]{2,1,0:T(8,128)}, f32[2,32,2048]{2,1,0:T(8,128)}, u32[]{:S(2)}, u32[]{:S(2)}) %collective-permute-start.1) | collective-permute-done | bytes 524320 | tf_op jit(solution)/shard_map/ppermute | solution.py:15
  22.9 3.2 %collective-permute-start.2 = (f32[2,2,32,512]{3,2,1,0:T(8,128)S(1)}, f32[2,2,32,512]{3,2,1,0:T(8,128)S(1)}, u32[]{:S(2)}, u32[]{:S(2)}) collective-permute-start(f32[2,2,32,512]{3,2,1,0:T(8,128)S(1)} %get-tuple-element.40), channel_id=1, source_target_pairs={{0,1},{1,2},{2,3},{4,5},{5,6},{6,7},{8,9},{9,10},{10,11},{12,13},{... | collective-permute-start | bytes 786440 | tf_op jit(solution)/shard_map/ppermute | solution.py:26
  29.9 3.3 %collective-permute-done.3 = f32[2,2,32,512]{3,2,1,0:T(8,128)S(1)} collective-permute-done((f32[2,2,32,512]{3,2,1,0:T(8,128)S(1)}, f32[2,2,32,512]{3,2,1,0:T(8,128)S(1)}, u32[]{:S(2)}, u32[]{:S(2)}) %collective-permute-start.3) | collective-permute-done | bytes 262176 | tf_op jit(solution)/shard_map/ppermute | solution.py:28
  56.4 3.2 %collective-permute-start.4 = (f32[2,32,2048]{2,1,0:T(8,128)S(1)}, f32[2,32,2048]{2,1,0:T(8,128)S(1)}, u32[]{:S(2)}, u32[]{:S(2)}) collective-permute-start(f32[2,32,2048]{2,1,0:T(8,128)S(1)} %get-tuple-element.38), channel_id=1, source_target_pairs={{0,4},{4,8},{8,12},{12,16},{16,20},{20,24},{24,28},{28,32},{32,36}... | collective-permute-start | bytes 1572872 | tf_op jit(solution)/shard_map/ppermute | solution.py:15
  61.5 4.2 %collective-permute-done.4 = f32[2,32,2048]{2,1,0:T(8,128)S(1)} collective-permute-done((f32[2,32,2048]{2,1,0:T(8,128)S(1)}, f32[2,32,2048]{2,1,0:T(8,128)S(1)}, u32[]{:S(2)}, u32[]{:S(2)}) %collective-permute-start.4) | collective-permute-done | bytes 524320 | tf_op jit(solution)/shard_map/ppermute | solution.py:15
  65.7 7.7 %collective-permute-done.5 = f32[2,32,2048]{2,1,0:T(8,128)S(1)} collective-permute-done((f32[2,32,2048]{2,1,0:T(8,128)S(1)}, f32[2,32,2048]{2,1,0:T(8,128)S(1)}, u32[]{:S(2)}, u32[]{:S(2)}) %collective-permute-start.5) | collective-permute-done | bytes 524320 | tf_op jit(solution)/shard_map/ppermute | solution.py:15
  73.4 3.2 %collective-permute-start.6 = (f32[2,2,32,512]{3,2,1,0:T(8,128)S(1)}, f32[2,2,32,512]{3,2,1,0:T(8,128)S(1)}, u32[]{:S(2)}, u32[]{:S(2)}) collective-permute-start(f32[2,2,32,512]{3,2,1,0:T(8,128)S(1)} %get-tuple-element.36), channel_id=1, source_target_pairs={{0,1},{1,2},{2,3},{4,5},{5,6},{6,7},{8,9},{9,10},{10,11},{12,13},{... | collective-permute-start | bytes 786440 | tf_op jit(solution)/shard_map/ppermute | solution.py:26
  79.9 3.8 %collective-permute-done.7 = f32[2,2,32,512]{3,2,1,0:T(8,128)S(1)} collective-permute-done((f32[2,2,32,512]{3,2,1,0:T(8,128)S(1)}, f32[2,2,32,512]{3,2,1,0:T(8,128)S(1)}, u32[]{:S(2)}, u32[]{:S(2)}) %collective-permute-start.7) | collective-permute-done | bytes 262176 | tf_op jit(solution)/shard_map/ppermute | solution.py:28
  96.6 2.9 %fusion.13 = f32[2,2,32,20,128]{4,2,1,0,3:T(8,128)S(1)} fusion(f32[1,20,2,128,128]{4,3,2,1,0:T(8,128)S(1)} %copy-done, f32[2,32,5,128]{3,1,0,2:T(8,128)S(1)} %select_bitcast_fusion.12, f32[2,32,5,128]{3,1,0,2:T(8,128)S(1)} %select_bitcast_fusion.13, f32[2,32,5,128]{3,1,0,2:T(8,128)S(1)} %select_bitcast_fusion.14, ...), kind=kOutput, calls=%fused_computation.36 | convolution fusion | flops 503808000 | bytes 4587520 | tf_op jit(solution)/shard_map/csnj,ndij->cdsni/dot_general | solution.py:36
  105.9 3.2 %collective-permute-start.8 = (f32[2,32,2048]{2,1,0:T(8,128)S(1)}, f32[2,32,2048]{2,1,0:T(8,128)S(1)}, u32[]{:S(2)}, u32[]{:S(2)}) collective-permute-start(f32[2,32,2048]{2,1,0:T(8,128)S(1)} %get-tuple-element.34), channel_id=1, source_target_pairs={{0,4},{4,8},{8,12},{12,16},{16,20},{20,24},{24,28},{28,32},{32,36}... | collective-permute-start | bytes 1572872 | tf_op jit(solution)/shard_map/ppermute | solution.py:15
  111.0 4.2 %collective-permute-done.8 = f32[2,32,2048]{2,1,0:T(8,128)S(1)} collective-permute-done((f32[2,32,2048]{2,1,0:T(8,128)S(1)}, f32[2,32,2048]{2,1,0:T(8,128)S(1)}, u32[]{:S(2)}, u32[]{:S(2)}) %collective-permute-start.8) | collective-permute-done | bytes 524320 | tf_op jit(solution)/shard_map/ppermute | solution.py:15
  115.1 7.7 %collective-permute-done.9 = f32[2,32,2048]{2,1,0:T(8,128)S(1)} collective-permute-done((f32[2,32,2048]{2,1,0:T(8,128)S(1)}, f32[2,32,2048]{2,1,0:T(8,128)S(1)}, u32[]{:S(2)}, u32[]{:S(2)}) %collective-permute-start.9) | collective-permute-done | bytes 524320 | tf_op jit(solution)/shard_map/ppermute | solution.py:15
  129.1 3.8 %collective-permute-done.11 = f32[2,2,32,512]{3,2,1,0:T(8,128)S(1)} collective-permute-done((f32[2,2,32,512]{3,2,1,0:T(8,128)S(1)}, f32[2,2,32,512]{3,2,1,0:T(8,128)S(1)}, u32[]{:S(2)}, u32[]{:S(2)}) %collective-permute-start.11) | collective-permute-done | bytes 262176 | tf_op jit(solution)/shard_map/ppermute | solution.py:28
  155.0 3.2 %collective-permute-start.12 = (f32[2,32,2048]{2,1,0:T(8,128)S(1)}, f32[2,32,2048]{2,1,0:T(8,128)S(1)}, u32[]{:S(2)}, u32[]{:S(2)}) collective-permute-start(f32[2,32,2048]{2,1,0:T(8,128)S(1)} %get-tuple-element.30), channel_id=1, source_target_pairs={{0,4},{4,8},{8,12},{12,16},{16,20},{20,24},{24,28},{28,32},{32,36}... | collective-permute-start | bytes 1572872 | tf_op jit(solution)/shard_map/ppermute | solution.py:15
  160.1 4.2 %collective-permute-done.12 = f32[2,32,2048]{2,1,0:T(8,128)S(1)} collective-permute-done((f32[2,32,2048]{2,1,0:T(8,128)S(1)}, f32[2,32,2048]{2,1,0:T(8,128)S(1)}, u32[]{:S(2)}, u32[]{:S(2)}) %collective-permute-start.12) | collective-permute-done | bytes 524320 | tf_op jit(solution)/shard_map/ppermute | solution.py:15
  164.3 7.7 %collective-permute-done.13 = f32[2,32,2048]{2,1,0:T(8,128)S(1)} collective-permute-done((f32[2,32,2048]{2,1,0:T(8,128)S(1)}, f32[2,32,2048]{2,1,0:T(8,128)S(1)}, u32[]{:S(2)}, u32[]{:S(2)}) %collective-permute-start.13) | collective-permute-done | bytes 524320 | tf_op jit(solution)/shard_map/ppermute | solution.py:15
  177.0 3.8 %collective-permute-done.15 = f32[2,2,32,512]{3,2,1,0:T(8,128)S(1)} collective-permute-done((f32[2,2,32,512]{3,2,1,0:T(8,128)S(1)}, f32[2,2,32,512]{3,2,1,0:T(8,128)S(1)}, u32[]{:S(2)}, u32[]{:S(2)}) %collective-permute-start.15) | collective-permute-done | bytes 262176 | tf_op jit(solution)/shard_map/ppermute | solution.py:28
  193.7 2.9 %fusion.19 = f32[2,2,32,20,128]{4,2,1,0,3:T(8,128)S(1)} fusion(f32[1,20,2,128,128]{4,3,2,1,0:T(8,128)S(1)} %copy-done, f32[2,32,5,128]{3,1,0,2:T(8,128)S(1)} %select_bitcast_fusion.4, f32[2,32,5,128]{3,1,0,2:T(8,128)S(1)} %select_bitcast_fusion.5, f32[2,32,5,128]{3,1,0,2:T(8,128)S(1)} %select_bitcast_fusion.6, f32[2,32,5,128]{3,1,0,2:T(8,128)S(1)} %select_bitcast_fusion.7), kind=kOutput, calls=%fused_computation.38 | convolution fusion | flops 503808000 | bytes 4587520 | tf_op jit(solution)/shard_map/csnj,ndij->cdsni/dot_general | solution.py:36
  203.0 3.2 %collective-permute-start.16 = (f32[2,32,2048]{2,1,0:T(8,128)S(1)}, f32[2,32,2048]{2,1,0:T(8,128)S(1)}, u32[]{:S(2)}, u32[]{:S(2)}) collective-permute-start(f32[2,32,2048]{2,1,0:T(8,128)S(1)} %get-tuple-element.26), channel_id=1, source_target_pairs={{0,4},{4,8},{8,12},{12,16},{16,20},{20,24},{24,28},{28,32},{32,36}... | collective-permute-start | bytes 1572872 | tf_op jit(solution)/shard_map/ppermute | solution.py:15
  208.1 4.2 %collective-permute-done.16 = f32[2,32,2048]{2,1,0:T(8,128)S(1)} collective-permute-done((f32[2,32,2048]{2,1,0:T(8,128)S(1)}, f32[2,32,2048]{2,1,0:T(8,128)S(1)}, u32[]{:S(2)}, u32[]{:S(2)}) %collective-permute-start.16) | collective-permute-done | bytes 524320 | tf_op jit(solution)/shard_map/ppermute | solution.py:15
  212.2 7.7 %collective-permute-done.17 = f32[2,32,2048]{2,1,0:T(8,128)S(1)} collective-permute-done((f32[2,32,2048]{2,1,0:T(8,128)S(1)}, f32[2,32,2048]{2,1,0:T(8,128)S(1)}, u32[]{:S(2)}, u32[]{:S(2)}) %collective-permute-start.17) | collective-permute-done | bytes 524320 | tf_op jit(solution)/shard_map/ppermute | solution.py:15
  224.9 3.8 %collective-permute-done.19 = f32[2,2,32,512]{3,2,1,0:T(8,128)S(1)} collective-permute-done((f32[2,2,32,512]{3,2,1,0:T(8,128)S(1)}, f32[2,2,32,512]{3,2,1,0:T(8,128)S(1)}, u32[]{:S(2)}, u32[]{:S(2)}) %collective-permute-start.19) | collective-permute-done | bytes 262176 | tf_op jit(solution)/shard_map/ppermute | solution.py:28
  (144 shorter events, 141.4 us)
Async XLA Ops:
  0.0 47.1 %copy-start = (f32[1,20,2,128,128]{4,3,2,1,0:T(8,128)S(1)}, f32[1,20,2,128,128]{4,3,2,1,0:T(8,128)}, u32[]{:S(2)}) copy-start(f32[1,20,2,128,128]{4,3,2,1,0:T(8,128)} %param.7) | copy-start | bytes 7864324
  0.0 9.6 %copy-start.2 = (s32[1,20,2]{1,2,0:T(2,128)S(1)}, s32[1,20,2]{1,2,0:T(2,128)}, u32[]{:S(2)}) copy-start(s32[1,20,2]{1,2,0:T(2,128)} %param.8) | copy-start | bytes 484
  0.0 9.8 %copy-start.1 = (s32[1,4]{1,0:T(1,128)S(1)}, s32[1,4]{1,0:T(1,128)}, u32[]{:S(2)}) copy-start(s32[1,4]{1,0:T(1,128)} %param.9) | copy-start | bytes 52
  2.5 11.6 %collective-permute-start = (f32[2,32,2048]{2,1,0:T(8,128)}, f32[2,32,2048]{2,1,0:T(8,128)S(1)}, u32[]{:S(2)}, u32[]{:S(2)}) collective-permute-start(f32[2,32,2048]{2,1,0:T(8,128)} %get-tuple-element.42), channel_id=1, source_target_pairs={{0,4},{4,8},{8,12},{12,16},{16,20},{20,24},{24,28},{28,32},{32,36}... | collective-permute-start | bytes 1572872 | tf_op jit(solution)/shard_map/ppermute | solution.py:15
  7.7 14.1 %collective-permute-start.1 = (f32[2,32,2048]{2,1,0:T(8,128)}, f32[2,32,2048]{2,1,0:T(8,128)}, u32[]{:S(2)}, u32[]{:S(2)}) collective-permute-start(f32[2,32,2048]{2,1,0:T(8,128)} %get-tuple-element.43), channel_id=1, source_target_pairs={{4,0},{8,4},{12,8},{16,12},{20,16},{24,20},{28,24},{32,28},{36,32}... | collective-permute-start | bytes 1572872 | tf_op jit(solution)/shard_map/ppermute | solution.py:15
  22.9 7.1 %collective-permute-start.2 = (f32[2,2,32,512]{3,2,1,0:T(8,128)S(1)}, f32[2,2,32,512]{3,2,1,0:T(8,128)S(1)}, u32[]{:S(2)}, u32[]{:S(2)}) collective-permute-start(f32[2,2,32,512]{3,2,1,0:T(8,128)S(1)} %get-tuple-element.40), channel_id=1, source_target_pairs={{0,1},{1,2},{2,3},{4,5},{5,6},{6,7},{8,9},{9,10},{10,11},{12,13},{... | collective-permute-start | bytes 786440 | tf_op jit(solution)/shard_map/ppermute | solution.py:26
  26.1 7.1 %collective-permute-start.3 = (f32[2,2,32,512]{3,2,1,0:T(8,128)S(1)}, f32[2,2,32,512]{3,2,1,0:T(8,128)S(1)}, u32[]{:S(2)}, u32[]{:S(2)}) collective-permute-start(f32[2,2,32,512]{3,2,1,0:T(8,128)S(1)} %get-tuple-element.41), channel_id=1, source_target_pairs={{1,0},{2,1},{3,2},{5,4},{6,5},{7,6},{9,8},{10,9},{11,10},{13,12},{... | collective-permute-start | bytes 786440 | tf_op jit(solution)/shard_map/ppermute | solution.py:28
  56.4 9.3 %collective-permute-start.4 = (f32[2,32,2048]{2,1,0:T(8,128)S(1)}, f32[2,32,2048]{2,1,0:T(8,128)S(1)}, u32[]{:S(2)}, u32[]{:S(2)}) collective-permute-start(f32[2,32,2048]{2,1,0:T(8,128)S(1)} %get-tuple-element.38), channel_id=1, source_target_pairs={{0,4},{4,8},{8,12},{12,16},{16,20},{20,24},{24,28},{28,32},{32,36}... | collective-permute-start | bytes 1572872 | tf_op jit(solution)/shard_map/ppermute | solution.py:15
  59.5 13.8 %collective-permute-start.5 = (f32[2,32,2048]{2,1,0:T(8,128)S(1)}, f32[2,32,2048]{2,1,0:T(8,128)S(1)}, u32[]{:S(2)}, u32[]{:S(2)}) collective-permute-start(f32[2,32,2048]{2,1,0:T(8,128)S(1)} %get-tuple-element.39), channel_id=1, source_target_pairs={{4,0},{8,4},{12,8},{16,12},{20,16},{24,20},{28,24},{32,28},{36,32}... | collective-permute-start | bytes 1572872 | tf_op jit(solution)/shard_map/ppermute | solution.py:15
  73.4 6.5 %collective-permute-start.6 = (f32[2,2,32,512]{3,2,1,0:T(8,128)S(1)}, f32[2,2,32,512]{3,2,1,0:T(8,128)S(1)}, u32[]{:S(2)}, u32[]{:S(2)}) collective-permute-start(f32[2,2,32,512]{3,2,1,0:T(8,128)S(1)} %get-tuple-element.36), channel_id=1, source_target_pairs={{0,1},{1,2},{2,3},{4,5},{5,6},{6,7},{8,9},{9,10},{10,11},{12,13},{... | collective-permute-start | bytes 786440 | tf_op jit(solution)/shard_map/ppermute | solution.py:26
  76.6 7.1 %collective-permute-start.7 = (f32[2,2,32,512]{3,2,1,0:T(8,128)S(1)}, f32[2,2,32,512]{3,2,1,0:T(8,128)S(1)}, u32[]{:S(2)}, u32[]{:S(2)}) collective-permute-start(f32[2,2,32,512]{3,2,1,0:T(8,128)S(1)} %get-tuple-element.37), channel_id=1, source_target_pairs={{1,0},{2,1},{3,2},{5,4},{6,5},{7,6},{9,8},{10,9},{11,10},{13,12},{... | collective-permute-start | bytes 786440 | tf_op jit(solution)/shard_map/ppermute | solution.py:28
  105.9 9.3 %collective-permute-start.8 = (f32[2,32,2048]{2,1,0:T(8,128)S(1)}, f32[2,32,2048]{2,1,0:T(8,128)S(1)}, u32[]{:S(2)}, u32[]{:S(2)}) collective-permute-start(f32[2,32,2048]{2,1,0:T(8,128)S(1)} %get-tuple-element.34), channel_id=1, source_target_pairs={{0,4},{4,8},{8,12},{12,16},{16,20},{20,24},{24,28},{28,32},{32,36}... | collective-permute-start | bytes 1572872 | tf_op jit(solution)/shard_map/ppermute | solution.py:15
  109.0 13.8 %collective-permute-start.9 = (f32[2,32,2048]{2,1,0:T(8,128)S(1)}, f32[2,32,2048]{2,1,0:T(8,128)S(1)}, u32[]{:S(2)}, u32[]{:S(2)}) collective-permute-start(f32[2,32,2048]{2,1,0:T(8,128)S(1)} %get-tuple-element.35), channel_id=1, source_target_pairs={{4,0},{8,4},{12,8},{16,12},{20,16},{24,20},{28,24},{32,28},{36,32}... | collective-permute-start | bytes 1572872 | tf_op jit(solution)/shard_map/ppermute | solution.py:15
  122.9 6.2 %collective-permute-start.10 = (f32[2,2,32,512]{3,2,1,0:T(8,128)S(1)}, f32[2,2,32,512]{3,2,1,0:T(8,128)S(1)}, u32[]{:S(2)}, u32[]{:S(2)}) collective-permute-start(f32[2,2,32,512]{3,2,1,0:T(8,128)S(1)} %get-tuple-element.32), channel_id=1, source_target_pairs={{0,1},{1,2},{2,3},{4,5},{5,6},{6,7},{8,9},{9,10},{10,11},{12,13},{... | collective-permute-start | bytes 786440 | tf_op jit(solution)/shard_map/ppermute | solution.py:26
  125.8 7.1 %collective-permute-start.11 = (f32[2,2,32,512]{3,2,1,0:T(8,128)S(1)}, f32[2,2,32,512]{3,2,1,0:T(8,128)S(1)}, u32[]{:S(2)}, u32[]{:S(2)}) collective-permute-start(f32[2,2,32,512]{3,2,1,0:T(8,128)S(1)} %get-tuple-element.33), channel_id=1, source_target_pairs={{1,0},{2,1},{3,2},{5,4},{6,5},{7,6},{9,8},{10,9},{11,10},{13,12},{... | collective-permute-start | bytes 786440 | tf_op jit(solution)/shard_map/ppermute | solution.py:28
  155.0 9.3 %collective-permute-start.12 = (f32[2,32,2048]{2,1,0:T(8,128)S(1)}, f32[2,32,2048]{2,1,0:T(8,128)S(1)}, u32[]{:S(2)}, u32[]{:S(2)}) collective-permute-start(f32[2,32,2048]{2,1,0:T(8,128)S(1)} %get-tuple-element.30), channel_id=1, source_target_pairs={{0,4},{4,8},{8,12},{12,16},{16,20},{20,24},{24,28},{28,32},{32,36}... | collective-permute-start | bytes 1572872 | tf_op jit(solution)/shard_map/ppermute | solution.py:15
  158.2 13.8 %collective-permute-start.13 = (f32[2,32,2048]{2,1,0:T(8,128)S(1)}, f32[2,32,2048]{2,1,0:T(8,128)S(1)}, u32[]{:S(2)}, u32[]{:S(2)}) collective-permute-start(f32[2,32,2048]{2,1,0:T(8,128)S(1)} %get-tuple-element.31), channel_id=1, source_target_pairs={{4,0},{8,4},{12,8},{16,12},{20,16},{24,20},{28,24},{32,28},{36,32}... | collective-permute-start | bytes 1572872 | tf_op jit(solution)/shard_map/ppermute | solution.py:15
  172.1 4.9 %collective-permute-start.14 = (f32[2,2,32,512]{3,2,1,0:T(8,128)S(1)}, f32[2,2,32,512]{3,2,1,0:T(8,128)S(1)}, u32[]{:S(2)}, u32[]{:S(2)}) collective-permute-start(f32[2,2,32,512]{3,2,1,0:T(8,128)S(1)} %get-tuple-element.28), channel_id=1, source_target_pairs={{0,1},{1,2},{2,3},{4,5},{5,6},{6,7},{8,9},{9,10},{10,11},{12,13},{... | collective-permute-start | bytes 786440 | tf_op jit(solution)/shard_map/ppermute | solution.py:26
  173.7 7.1 %collective-permute-start.15 = (f32[2,2,32,512]{3,2,1,0:T(8,128)S(1)}, f32[2,2,32,512]{3,2,1,0:T(8,128)S(1)}, u32[]{:S(2)}, u32[]{:S(2)}) collective-permute-start(f32[2,2,32,512]{3,2,1,0:T(8,128)S(1)} %get-tuple-element.29), channel_id=1, source_target_pairs={{1,0},{2,1},{3,2},{5,4},{6,5},{7,6},{9,8},{10,9},{11,10},{13,12},{... | collective-permute-start | bytes 786440 | tf_op jit(solution)/shard_map/ppermute | solution.py:28
  203.0 9.3 %collective-permute-start.16 = (f32[2,32,2048]{2,1,0:T(8,128)S(1)}, f32[2,32,2048]{2,1,0:T(8,128)S(1)}, u32[]{:S(2)}, u32[]{:S(2)}) collective-permute-start(f32[2,32,2048]{2,1,0:T(8,128)S(1)} %get-tuple-element.26), channel_id=1, source_target_pairs={{0,4},{4,8},{8,12},{12,16},{16,20},{20,24},{24,28},{28,32},{32,36}... | collective-permute-start | bytes 1572872 | tf_op jit(solution)/shard_map/ppermute | solution.py:15
  206.1 13.8 %collective-permute-start.17 = (f32[2,32,2048]{2,1,0:T(8,128)S(1)}, f32[2,32,2048]{2,1,0:T(8,128)S(1)}, u32[]{:S(2)}, u32[]{:S(2)}) collective-permute-start(f32[2,32,2048]{2,1,0:T(8,128)S(1)} %get-tuple-element.27), channel_id=1, source_target_pairs={{4,0},{8,4},{12,8},{16,12},{20,16},{24,20},{28,24},{32,28},{36,32}... | collective-permute-start | bytes 1572872 | tf_op jit(solution)/shard_map/ppermute | solution.py:15
  220.0 4.9 %collective-permute-start.18 = (f32[2,2,32,512]{3,2,1,0:T(8,128)S(1)}, f32[2,2,32,512]{3,2,1,0:T(8,128)S(1)}, u32[]{:S(2)}, u32[]{:S(2)}) collective-permute-start(f32[2,2,32,512]{3,2,1,0:T(8,128)S(1)} %get-tuple-element.24), channel_id=1, source_target_pairs={{0,1},{1,2},{2,3},{4,5},{5,6},{6,7},{8,9},{9,10},{10,11},{12,13},{... | collective-permute-start | bytes 786440 | tf_op jit(solution)/shard_map/ppermute | solution.py:26
  221.6 7.1 %collective-permute-start.19 = (f32[2,2,32,512]{3,2,1,0:T(8,128)S(1)}, f32[2,2,32,512]{3,2,1,0:T(8,128)S(1)}, u32[]{:S(2)}, u32[]{:S(2)}) collective-permute-start(f32[2,2,32,512]{3,2,1,0:T(8,128)S(1)} %get-tuple-element.25), channel_id=1, source_target_pairs={{1,0},{2,1},{3,2},{5,4},{6,5},{7,6},{9,8},{10,9},{11,10},{13,12},{... | collective-permute-start | bytes 786440 | tf_op jit(solution)/shard_map/ppermute | solution.py:28
where the time goes:
time: 252 us; the launch traced here: 250 us
  waiting for transfers between devices  85.1 us (34%)
  local copies, waits for them, and re-layouts  59 us (23%)
  starting transfers between devices  47 us (19%)
  other arithmetic  33.4 us (13%)
  matrix products  24.7 us (10%)
    ppermute x10, waiting for transfers between devices, from_behind(): return lax.ppermute(block, axis, route)  59 us
    gather x20, local copies, waits for them, and re-layouts, padded_update(): picks.append(jnp.take(tiled[anchor], columns, axis=2))  35.7 us
    ppermute x10, starting transfers between devices, from_behind(): return lax.ppermute(block, axis, route)  27.5 us
    ppermute x5, waiting for transfers between devices, padded(): lax.ppermute(head, axis, [((i + 1) % count, i) for i in range(ends)])  18.6 us
    select_n x18, other arithmetic, padded_update(): picks.append(jnp.take(tiled[anchor], columns, axis=2))  18.1 us
    dot_general x5, matrix products, complex_term(): prod = jnp.einsum(pattern, picked, blocks, precision=lax.Precision.HIGHEST)  14.7 us
    ppermute x5, starting transfers between devices, padded(): lax.ppermute(tail, axis, [(i, (i + 1) % count) for i in range(ends)])  12.6 us
    reshape x5, local copies, waits for them, and re-layouts, body(): waves = local_sources + update.reshape(2, 2, shots, width)  11.9 us
  transfers between devices with their start and end apart: 20, of which 19 were waited for; matrix products, arithmetic and copies ran while one was open for 1% of the time, Pallas kernels for 0%

commit v1 on v0

v1 whole, which is shorter than its diff:
```python
import functools

import jax
import jax.numpy as jnp
from jax import lax
from jax.experimental import pallas as pl
from jax.experimental.pallas import tpu as pltpu
from jax.sharding import PartitionSpec as P

TILE = 128
CAP = 5
BAND = 4
SWEEPS = 5
TILES_DEV = 16
LIVE = 10
OWN = (8, 7)
GROUP = 8
SRC = LIVE
MESH = pl.DeviceIdType.MESH
F32 = jnp.float32
BF16 = jnp.bfloat16


def reader_columns(meta, first_kind, second_kind, count):
    starts = [meta[2 * LIVE * 2 + k] for k in (first_kind, second_kind)]
    columns = []
    for e in range(count):
        in_first = e < starts[0]
        slot_first = first_kind * CAP + min(e, CAP - 1)
        slot_second = second_kind * CAP + jnp.clip(e - starts[0], 0, CAP - 1)
        slot = jnp.where(in_first, slot_first, slot_second)
        columns.append(meta[2 * slot + 1])
    return columns


def kernel(
    layers,
    tile_devs,
    groups,
    meta,
    src_hbm,
    green_hbm,
    out_hbm,
    state,
    recv,
    send,
    stage,
    weights,
    green,
    final,
    meta_next,
    meta_prev,
    slot_of,
    entry_of,
    source_of,
    same,
    where_is,
    pack_of,
    local_sem,
    out_sem,
    meta_send_sem,
    meta_recv_sem,
    send_sem,
    recv_sem,
):
    layer = lax.axis_index("layer")
    place = lax.axis_index("tile")
    up_ok, down_ok = layer > 0, layer < layers - 1
    low_ok, high_ok = place > 0, place < tile_devs - 1

    src_copies = []
    for direction in range(2):
        for tile in range(TILES_DEV):
            copy = pltpu.make_async_copy(
                src_hbm.at[direction, :, :, pl.ds(tile * TILE, TILE)],
                state.at[SRC + direction * TILES_DEV + tile],
                local_sem.at[direction * TILES_DEV + tile],
            )
            copy.start()
            src_copies.append(copy)
    green_copy = pltpu.make_async_copy(green_hbm, green, local_sem.at[2 * TILES_DEV])
    green_copy.start()

    @pl.when(layer == 0)
    def _():
        @pl.loop(0, SWEEPS * groups)
        def _(i):
            recv[i // groups, i % groups, pl.ds(0, 16)] = jnp.zeros((16, 2, GROUP, TILE), F32)

    @pl.when(layer == layers - 1)
    def _():
        @pl.loop(0, SWEEPS * groups)
        def _(i):
            recv[i // groups, i % groups, pl.ds(16, 16)] = jnp.zeros((16, 2, GROUP, TILE), F32)

    lower, upper = layer + 1, layer - 1
    links = [
        (down_ok, (lower, place), up_ok),
        (down_ok & low_ok, (lower, place - 1), up_ok & high_ok),
        (down_ok & high_ok, (lower, place + 1), up_ok & low_ok),
        (up_ok, (upper, place), down_ok),
        (up_ok & low_ok, (upper, place - 1), down_ok & high_ok),
        (up_ok & high_ok, (upper, place + 1), down_ok & low_ok),
    ]

    barrier = pltpu.get_barrier_semaphore()
    for ok, device, _ in links:

        @pl.when(ok)
        def _(device=device):
            pl.semaphore_signal(barrier, inc=1, device_id=device, device_id_type=MESH)

    sides = 1 + low_ok.astype(jnp.int32) + high_ok.astype(jnp.int32)
    ends = up_ok.astype(jnp.int32) + down_ok.astype(jnp.int32)
    pl.semaphore_wait(barrier, sides * ends)

    to_prev = pltpu.make_async_remote_copy(
        meta, meta_next, meta_send_sem.at[0], meta_recv_sem.at[0], device_id=(upper, place), device_id_type=MESH
    )
    to_next = pltpu.make_async_remote_copy(
        meta, meta_prev, meta_send_sem.at[1], meta_recv_sem.at[1], device_id=(lower, place), device_id_type=MESH
    )

    @pl.when(up_ok)
    def _():
        to_prev.start()

    @pl.when(down_ok)
    def _():
        to_next.start()

    def message(k, g, q):
        direction, kind = q // 3, q % 3
        base = direction * 16
        count = OWN[direction] if kind == 0 else BAND
        if kind == 0:
            source = send.at[k, g, pl.ds(base, count)]
            target = base
        elif kind == 1:
            source = send.at[k, g, pl.ds(base + 8, count)]
            target = base + 12
        else:
            source = send.at[k, g, pl.ds(base + 12, count)]
            target = base + 8
        return pltpu.make_async_remote_copy(
            source,
            recv.at[k, g, pl.ds(target, count)],
            send_sem.at[k, g, q],
            recv_sem.at[k, g, q],
            device_id=links[q][1],
            device_id_type=MESH,
        )

    def first_halo(g, q):
        direction, kind = q // 3, q % 3
        base = direction * 16
        tile = SRC + base + (0 if kind == 1 else TILES_DEV - BAND)
        target = base + (12 if kind == 1 else 8)
        return pltpu.make_async_remote_copy(
            state.at[pl.ds(tile, BAND), :, pl.ds(pl.multiple_of(g * GROUP, GROUP), GROUP), :],
            recv.at[0, g, pl.ds(target, BAND)],
            send_sem.at[0, g, q],
            recv_sem.at[0, g, q],
            device_id=links[q][1],
            device_id_type=MESH,
        )

    for copy in src_copies:
        copy.wait()
    for g in range(groups):
        for q in (1, 2, 4, 5):

            @pl.when(links[q][0])
            def _(g=g, q=q):
                first_halo(g, q).start()

    c0, c1, c2, c3 = [meta[2 * LIVE * 2 + k] for k in range(4)]
    p1, p2, p3 = c0, c0 + c1, c0 + c1 + c2
    total = p3 + c3
    targets, lives = [], []
    for j in range(LIVE):
        in1, in2, in3 = j >= p1, j >= p2, j >= p3
        kind = in1.astype(jnp.int32) + in2.astype(jnp.int32) + in3.astype(jnp.int32)
        base = jnp.where(in3, p3, jnp.where(in2, p2, jnp.where(in1, p1, 0)))
        live = j < total
        slot = jnp.where(live, kind * CAP + j - base, 0)
        row = meta[2 * slot] - place * TILES_DEV
        col = meta[2 * slot + 1] - place * TILES_DEV
        reads_up = in1 & jnp.logical_not(in3)
        own = j - base + jnp.where(in3, c0, jnp.where(in2, c1, 0))
        entry = jnp.where(col < 0, 8 + BAND + col, jnp.where(col >= TILES_DEV, 12 + col - TILES_DEV, own))
        entry = entry + jnp.where(reads_up, 16, 0)
        target = row + jnp.where(in2, TILES_DEV, 0)
        slot_of[j] = slot
        entry_of[j] = jnp.where(live, entry, 0)
        source_of[j] = SRC + jnp.where(live, target, 0)
        targets.append(jnp.where(live, target, 64 + j))
        lives.append(live)
    for j in range(LIVE):
        same[j, j] = jnp.where(lives[j], 1.0, 0.0)
        for i in range(j):
            same[j, i] = jnp.where(targets[j] == targets[i], 1.0, 0.0)
    for r in range(2 * TILES_DEV):
        found = SRC + r
        for j in range(LIVE):
            found = jnp.where(targets[j] == r, j, found)
        where_is[r] = found

    @pl.when(up_ok)
    def _():
        to_prev.wait_send()
        to_next_recv = pltpu.make_async_remote_copy(
            meta, meta_prev, meta_send_sem.at[1], meta_recv_sem.at[1], device_id=(upper, place), device_id_type=MESH
        )
        to_next_recv.wait_recv()
        for e, column in enumerate(reader_columns(meta_prev, 1, 2, OWN[1])):
            pack_of[16 + e] = TILES_DEV + jnp.clip(column - place * TILES_DEV, 0, TILES_DEV - 1)

    @pl.when(down_ok)
    def _():
        to_next.wait_send()
        to_prev_recv = pltpu.make_async_remote_copy(
            meta, meta_next, meta_send_sem.at[0], meta_recv_sem.at[0], device_id=(lower, place), device_id_type=MESH
        )
        to_prev_recv.wait_recv()
        for e, column in enumerate(reader_columns(meta_next, 0, 3, OWN[0])):
            pack_of[e] = jnp.clip(column - place * TILES_DEV, 0, TILES_DEV - 1)

    def shots_of(g):
        return pl.ds(pl.multiple_of(g * GROUP, GROUP), GROUP)

    def pack_own(k, g, index_of):
        for direction, ok in ((0, down_ok), (1, up_ok)):

            @pl.when(ok)
            def _(direction=direction):
                for e in range(OWN[direction]):
                    i = direction * 16 + e
                    send[k, g, i] = state[index_of(pack_of[i]), :, shots_of(g), :]
                message(k, g, direction * 3).start()

    @pl.loop(0, groups)
    def _(g):
        pack_own(0, g, lambda tile: SRC + tile)

    green_copy.wait()

    @pl.loop(0, LIVE)
    def _(j):
        blocks = green[slot_of[j]] * jnp.where(j < total, 1.0, 0.0)
        re, im = blocks[0], blocks[1]
        for part, (row, col) in ((re, (0, 0)), (-im, (0, 1)), (im, (1, 0)), (re, (1, 1))):
            high = part.astype(BF16)
            low = (part - high.astype(F32)).astype(BF16)
            weights[j, pl.ds(row * TILE, TILE), pl.ds(col * TILE, TILE)] = high
            weights[j, pl.ds((2 + row) * TILE, TILE), pl.ds(col * TILE, TILE)] = low

    def step(k, g):
        for q in range(6):

            @pl.when(links[q][2])
            def _(q=q):
                message(k, g, q).wait_recv()

        stage[...] = recv[k, g]
        terms = []
        for j in range(LIVE):
            x = stage[entry_of[j]]
            x = jnp.concatenate([x[0], x[1]], axis=1)
            high = x.astype(BF16).astype(F32)
            both = jnp.concatenate([high, x - high], axis=0).astype(BF16)
            p = lax.dot_general(both, weights[j], (((1,), (1,)), ((), ())), preferred_element_type=F32)
            p = p[:, : 2 * TILE] + p[:, 2 * TILE :]
            terms.append(p[:GROUP] + p[GROUP:])
        for j in range(LIVE):
            acc = terms[j]
            for i in range(j):
                acc = acc + same[j, i] * terms[i]
            at = source_of[j]
            state[j, 0, shots_of(g), :] = acc[:, :TILE] + state[at, 0, shots_of(g), :]
            state[j, 1, shots_of(g), :] = acc[:, TILE:] + state[at, 1, shots_of(g), :]

        @pl.when(k < SWEEPS - 1)
        def _():
            for q in (1, 2, 4, 5):
                direction, kind = q // 3, q % 3

                @pl.when(links[q][0])
                def _(q=q, direction=direction, kind=kind):
                    first = 0 if kind == 1 else TILES_DEV - BAND
                    for e in range(BAND):
                        found = where_is[direction * TILES_DEV + first + e]
                        send[k + 1, g, direction * 16 + 4 + 4 * kind + e] = state[found, :, shots_of(g), :]
                    message(k + 1, g, q).start()

            pack_own(k + 1, g, lambda tile: where_is[tile])

        @pl.when(k == SWEEPS - 1)
        def _():
            for r in range(2 * TILES_DEV):
                final[r, :, shots_of(g), :] = state[where_is[r], :, shots_of(g), :]

    @pl.loop(0, SWEEPS * groups)
    def _(i):
        step(i // groups, i % groups)

    out_copies = []
    for r in range(2 * TILES_DEV):
        copy = pltpu.make_async_copy(
            final.at[r],
            out_hbm.at[r // TILES_DEV, :, :, pl.ds(r % TILES_DEV * TILE, TILE)],
            out_sem.at[r],
        )
        copy.start()
        out_copies.append(copy)

    @pl.loop(0, SWEEPS * groups)
    def _(i):
        for q in range(6):

            @pl.when(links[q][0])
            def _(q=q):
                message(i // groups, i % groups, q).wait_send()

    for copy in out_copies:
        copy.wait()


def body(layers, tile_devs, sources, green, rowcol, counts):
    shots, width = sources.shape[3], sources.shape[4]
    groups = shots // GROUP
    slots = green.shape[1]
    meta = jnp.concatenate([rowcol.reshape(-1), counts.reshape(-1)])
    meta = jnp.pad(meta, (0, 128 - meta.shape[0]))
    any_space = pl.BlockSpec(memory_space=pl.ANY)
    out = pl.pallas_call(
        functools.partial(kernel, layers, tile_devs, groups),
        out_shape=jax.ShapeDtypeStruct((2, 2, shots, width), F32),
        in_specs=[pl.BlockSpec(memory_space=pltpu.SMEM), any_space, any_space],
        out_specs=any_space,
        scratch_shapes=[
            pltpu.VMEM((LIVE + 2 * TILES_DEV, 2, shots, TILE), F32),
            pltpu.VMEM((SWEEPS, groups, 32, 2, GROUP, TILE), F32),
            pltpu.VMEM((SWEEPS, groups, 32, 2, GROUP, TILE), F32),
            pltpu.VMEM((32, 2, GROUP, TILE), F32),
            pltpu.VMEM((LIVE, 4 * TILE, 2 * TILE), BF16),
            pltpu.VMEM((slots, 2, TILE, TILE), F32),
            pltpu.VMEM((2 * TILES_DEV, 2, shots, TILE), F32),
            pltpu.SMEM((128,), jnp.int32),
            pltpu.SMEM((128,), jnp.int32),
            pltpu.SMEM((LIVE,), jnp.int32),
            pltpu.SMEM((LIVE,), jnp.int32),
            pltpu.SMEM((LIVE,), jnp.int32),
            pltpu.SMEM((LIVE, LIVE), F32),
            pltpu.SMEM((2 * TILES_DEV,), jnp.int32),
            pltpu.SMEM((32,), jnp.int32),
            pltpu.SemaphoreType.DMA((2 * TILES_DEV + 1,)),
            pltpu.SemaphoreType.DMA((2 * TILES_DEV,)),
            pltpu.SemaphoreType.DMA((2,)),
            pltpu.SemaphoreType.DMA((2,)),
            pltpu.SemaphoreType.DMA((SWEEPS, groups, 6)),
            pltpu.SemaphoreType.DMA((SWEEPS, groups, 6)),
        ],
        compiler_params=pltpu.CompilerParams(collective_id=0, has_side_effects=True),
    )(meta, sources[0], green[0])
    return out[None]


def solution(mesh):
    return jax.shard_map(
        functools.partial(body, mesh.shape["layer"], mesh.shape["tile"]),
        mesh=mesh,
        in_specs=(
            P("layer", None, None, None, "tile"),
            P("layer", "tile", None, None, None),
            P("layer", "tile", None),
            P("layer", "tile"),
        ),
        out_specs=P("layer", None, None, None, "tile"),
        check_vma=False,
    )
```

time: 252 us -> 51.9 us (0.21)
  the two profiles are of different devices: /device:TPU:103 before, /device:TPU:392 now
where the time goes in v1:
time: 51.9 us; the launch traced here: 51.7 us
  Pallas kernels  47.3 us (91%)
  local copies, waits for them, and re-layouts  3.67 us (7%)
  other arithmetic  0.73 us (1%)
    pallas_call x1, Pallas kernels, body(): pl.pallas_call(functools.partial(kernel, layers, tile_devs, groups), out_...  47.3 us
    unnamed x2, local copies, waits for them, and re-layouts  3.06 us

profile of v1, /device:TPU:392, one launch (start us, length us, event | category | flops | bytes accessed | tf_op | source)
XLA Modules:
  0.0 51.7 jit_solution(824558969827592297)
XLA Ops:
  0.0 0.8 %copy.6 = s32[1,20,2]{2,1,0:T(8,128)S(1)} copy(s32[1,20,2]{1,2,0:T(2,128)} %param.6) | data formatting | bytes 320 | tf_op args[2]
  0.8 0.1 reshape.6
  0.9 0.7 %pad_add_fusion = s32[44]{0:T(128)S(1)} fusion(s32[4]{0:T(128)} %bitcast.7, s32[40]{0:T(128)S(1)} %reshape.6), kind=kLoop, calls=%fused_computation | loop fusion | flops 44 | bytes 352 | tf_op jit(solution)/shard_map/concatenate | solution.py:333
  1.6 0.5 pad.4.meta
  2.1 47.3 %shard_map.46 = f32[2,2,32,2048]{3,2,1,0:T(8,128)} custom-call(s32[128]{0:T(128)} %pad.4.meta, f32[2,2,32,2048]{3,2,1,0:T(8,128)} %bitcast.6, f32[20,2,128,128]{3,2,1,0:T(8,128)} %bitcast.5), custom_call_target="tpu_custom_call" | custom-call | tf_op jit(solution)/shard_map/pallas_call | solution.py:336
  49.4 2.3 %copy.8 = f32[1,2,2,32,2048]{4,3,2,1,0:T(8,128)} copy(f32[1,2,2,32,2048]{4,3,2,1,0:T(8,128)} %bitcast.4) | data formatting | bytes 2097152

commit v2 on v1

--- a/solution.py
+++ b/solution.py
@@ -17,19 +17,18 @@
 GROUP = 8
 SRC = LIVE
 MESH = pl.DeviceIdType.MESH
+VMEM = 24 << 20
 F32 = jnp.float32
 BF16 = jnp.bfloat16
 
 
-def reader_columns(meta, first_kind, second_kind, count):
-    starts = [meta[2 * LIVE * 2 + k] for k in (first_kind, second_kind)]
+def reader_columns(rowcol, counts, first_kind, second_kind, count):
+    first = counts[first_kind]
     columns = []
     for e in range(count):
-        in_first = e < starts[0]
         slot_first = first_kind * CAP + min(e, CAP - 1)
-        slot_second = second_kind * CAP + jnp.clip(e - starts[0], 0, CAP - 1)
-        slot = jnp.where(in_first, slot_first, slot_second)
-        columns.append(meta[2 * slot + 1])
+        slot_second = second_kind * CAP + jnp.clip(e - first, 0, CAP - 1)
+        columns.append(rowcol[1, jnp.where(e < first, slot_first, slot_second)])
     return columns
 
 
@@ -37,19 +36,23 @@
     layers,
     tile_devs,
     groups,
-    meta,
+    rowcol_hbm,
+    counts_hbm,
     src_hbm,
     green_hbm,
-    out_hbm,
+    out,
     state,
     recv,
     send,
     stage,
     weights,
     green,
-    final,
-    meta_next,
-    meta_prev,
+    rowcol,
+    counts,
+    cols_next,
+    counts_next,
+    cols_prev,
+    counts_prev,
     slot_of,
     entry_of,
     source_of,
@@ -57,7 +60,6 @@
     where_is,
     pack_of,
     local_sem,
-    out_sem,
     meta_send_sem,
     meta_recv_sem,
     send_sem,
@@ -68,6 +70,29 @@
     up_ok, down_ok = layer > 0, layer < layers - 1
     low_ok, high_ok = place > 0, place < tile_devs - 1
 
+    lower, upper = layer + 1, layer - 1
+    links = [
+        (down_ok, (lower, place), up_ok),
+        (down_ok & low_ok, (lower, place - 1), up_ok & high_ok),
+        (down_ok & high_ok, (lower, place + 1), up_ok & low_ok),
+        (up_ok, (upper, place), down_ok),
+        (up_ok & low_ok, (upper, place - 1), down_ok & high_ok),
+        (up_ok & high_ok, (upper, place + 1), down_ok & low_ok),
+    ]
+
+    barrier = pltpu.get_barrier_semaphore()
+    for ok, device, _ in links:
+
+        @pl.when(ok)
+        def _(device=device):
+            pl.semaphore_signal(barrier, inc=1, device_id=device, device_id_type=MESH)
+
+    list_copies = [
+        pltpu.make_async_copy(there, here, local_sem.at[2 * TILES_DEV + 1 + i])
+        for i, (there, here) in enumerate(((rowcol_hbm, rowcol), (counts_hbm, counts)))
+    ]
+    for copy in list_copies:
+        copy.start()
     src_copies = []
     for direction in range(2):
         for tile in range(TILES_DEV):
@@ -93,41 +118,35 @@
         def _(i):
             recv[i // groups, i % groups, pl.ds(16, 16)] = jnp.zeros((16, 2, GROUP, TILE), F32)
 
-    lower, upper = layer + 1, layer - 1
-    links = [
-        (down_ok, (lower, place), up_ok),
-        (down_ok & low_ok, (lower, place - 1), up_ok & high_ok),
-        (down_ok & high_ok, (lower, place + 1), up_ok & low_ok),
-        (up_ok, (upper, place), down_ok),
-        (up_ok & low_ok, (upper, place - 1), down_ok & high_ok),
-        (up_ok & high_ok, (upper, place + 1), down_ok & low_ok),
-    ]
-
-    barrier = pltpu.get_barrier_semaphore()
-    for ok, device, _ in links:
-
-        @pl.when(ok)
-        def _(device=device):
-            pl.semaphore_signal(barrier, inc=1, device_id=device, device_id_type=MESH)
-
     sides = 1 + low_ok.astype(jnp.int32) + high_ok.astype(jnp.int32)
     ends = up_ok.astype(jnp.int32) + down_ok.astype(jnp.int32)
+    for copy in list_copies:
+        copy.wait()
     pl.semaphore_wait(barrier, sides * ends)
 
-    to_prev = pltpu.make_async_remote_copy(
-        meta, meta_next, meta_send_sem.at[0], meta_recv_sem.at[0], device_id=(upper, place), device_id_type=MESH
-    )
-    to_next = pltpu.make_async_remote_copy(
-        meta, meta_prev, meta_send_sem.at[1], meta_recv_sem.at[1], device_id=(lower, place), device_id_type=MESH
-    )
+    def slot_lists(side, device):
+        there = ((cols_next, counts_next), (cols_prev, counts_prev))[side]
+        return [
+            pltpu.make_async_remote_copy(
+                here,
+                there[i],
+                meta_send_sem.at[side, i],
+                meta_recv_sem.at[side, i],
+                device_id=(device, place),
+                device_id_type=MESH,
+            )
+            for i, here in enumerate((rowcol, counts))
+        ]
 
     @pl.when(up_ok)
     def _():
-        to_prev.start()
+        for copy in slot_lists(0, upper):
+            copy.start()
 
     @pl.when(down_ok)
     def _():
-        to_next.start()
+        for copy in slot_lists(1, lower):
+            copy.start()
 
     def message(k, g, q):
         direction, kind = q // 3, q % 3
@@ -174,7 +193,7 @@
             def _(g=g, q=q):
                 first_halo(g, q).start()
 
-    c0, c1, c2, c3 = [meta[2 * LIVE * 2 + k] for k in range(4)]
+    c0, c1, c2, c3 = [counts[k] for k in range(4)]
     p1, p2, p3 = c0, c0 + c1, c0 + c1 + c2
     total = p3 + c3
     targets, lives = [], []
@@ -184,8 +203,8 @@
         base = jnp.where(in3, p3, jnp.where(in2, p2, jnp.where(in1, p1, 0)))
         live = j < total
         slot = jnp.where(live, kind * CAP + j - base, 0)
-        row = meta[2 * slot] - place * TILES_DEV
-        col = meta[2 * slot + 1] - place * TILES_DEV
+        row = rowcol[0, slot] - place * TILES_DEV
+        col = rowcol[1, slot] - place * TILES_DEV
         reads_up = in1 & jnp.logical_not(in3)
         own = j - base + jnp.where(in3, c0, jnp.where(in2, c1, 0))
         entry = jnp.where(col < 0, 8 + BAND + col, jnp.where(col >= TILES_DEV, 12 + col - TILES_DEV, own))
@@ -208,22 +227,20 @@
 
     @pl.when(up_ok)
     def _():
-        to_prev.wait_send()
-        to_next_recv = pltpu.make_async_remote_copy(
-            meta, meta_prev, meta_send_sem.at[1], meta_recv_sem.at[1], device_id=(upper, place), device_id_type=MESH
-        )
-        to_next_recv.wait_recv()
-        for e, column in enumerate(reader_columns(meta_prev, 1, 2, OWN[1])):
+        for copy in slot_lists(0, upper):
+            copy.wait_send()
+        for copy in slot_lists(1, upper):
+            copy.wait_recv()
+        for e, column in enumerate(reader_columns(cols_prev, counts_prev, 1, 2, OWN[1])):
             pack_of[16 + e] = TILES_DEV + jnp.clip(column - place * TILES_DEV, 0, TILES_DEV - 1)
 
     @pl.when(down_ok)
     def _():
-        to_next.wait_send()
-        to_prev_recv = pltpu.make_async_remote_copy(
-            meta, meta_next, meta_send_sem.at[0], meta_recv_sem.at[0], device_id=(lower, place), device_id_type=MESH
-        )
-        to_prev_recv.wait_recv()
-        for e, column in enumerate(reader_columns(meta_next, 0, 3, OWN[0])):
+        for copy in slot_lists(1, lower):
+            copy.wait_send()
+        for copy in slot_lists(0, lower):
+            copy.wait_recv()
+        for e, column in enumerate(reader_columns(cols_next, counts_next, 0, 3, OWN[0])):
             pack_of[e] = jnp.clip(column - place * TILES_DEV, 0, TILES_DEV - 1)
 
     def shots_of(g):
@@ -249,11 +266,10 @@
     def _(j):
         blocks = green[slot_of[j]] * jnp.where(j < total, 1.0, 0.0)
         re, im = blocks[0], blocks[1]
-        for part, (row, col) in ((re, (0, 0)), (-im, (0, 1)), (im, (1, 0)), (re, (1, 1))):
+        for row, part in enumerate((re, im)):
             high = part.astype(BF16)
-            low = (part - high.astype(F32)).astype(BF16)
-            weights[j, pl.ds(row * TILE, TILE), pl.ds(col * TILE, TILE)] = high
-            weights[j, pl.ds((2 + row) * TILE, TILE), pl.ds(col * TILE, TILE)] = low
+            weights[j, pl.ds(row * TILE, TILE)] = high
+            weights[j, pl.ds((2 + row) * TILE, TILE)] = (part - high.astype(F32)).astype(BF16)
 
     def step(k, g):
         for q in range(6):
@@ -266,19 +282,21 @@
         terms = []
         for j in range(LIVE):
             x = stage[entry_of[j]]
-            x = jnp.concatenate([x[0], x[1]], axis=1)
-            high = x.astype(BF16).astype(F32)
-            both = jnp.concatenate([high, x - high], axis=0).astype(BF16)
+            x = x.reshape(2 * GROUP, TILE)
+            high = x.astype(BF16)
+            both = jnp.concatenate([high, (x - high.astype(F32)).astype(BF16)], axis=0)
             p = lax.dot_general(both, weights[j], (((1,), (1,)), ((), ())), preferred_element_type=F32)
             p = p[:, : 2 * TILE] + p[:, 2 * TILE :]
-            terms.append(p[:GROUP] + p[GROUP:])
+            p = p[: 2 * GROUP] + p[2 * GROUP :]
+            by_re, by_im = p[:, :TILE], p[:, TILE:]
+            terms.append((by_re[:GROUP] - by_im[GROUP:], by_im[:GROUP] + by_re[GROUP:]))
         for j in range(LIVE):
-            acc = terms[j]
-            for i in range(j):
-                acc = acc + same[j, i] * terms[i]
             at = source_of[j]
-            state[j, 0, shots_of(g), :] = acc[:, :TILE] + state[at, 0, shots_of(g), :]
-            state[j, 1, shots_of(g), :] = acc[:, TILE:] + state[at, 1, shots_of(g), :]
+            for part in range(2):
+                acc = terms[j][part] + state[at, part, shots_of(g), :]
+                for i in range(j):
+                    acc = acc + same[j, i] * terms[i][part]
+                state[j, part, shots_of(g), :] = acc
 
         @pl.when(k < SWEEPS - 1)
         def _():
@@ -298,22 +316,13 @@
         @pl.when(k == SWEEPS - 1)
         def _():
             for r in range(2 * TILES_DEV):
-                final[r, :, shots_of(g), :] = state[where_is[r], :, shots_of(g), :]
+                columns = pl.ds(r % TILES_DEV * TILE, TILE)
+                out[r // TILES_DEV, :, shots_of(g), columns] = state[where_is[r], :, shots_of(g), :]
 
     @pl.loop(0, SWEEPS * groups)
     def _(i):
         step(i // groups, i % groups)
 
-    out_copies = []
-    for r in range(2 * TILES_DEV):
-        copy = pltpu.make_async_copy(
-            final.at[r],
-            out_hbm.at[r // TILES_DEV, :, :, pl.ds(r % TILES_DEV * TILE, TILE)],
-            out_sem.at[r],
-        )
-        copy.start()
-        out_copies.append(copy)
-
     @pl.loop(0, SWEEPS * groups)
     def _(i):
         for q in range(6):
@@ -322,47 +331,58 @@
             def _(q=q):
                 message(i // groups, i % groups, q).wait_send()
 
-    for copy in out_copies:
-        copy.wait()
+
+def put_out(there, out, sem):
+    copy = pltpu.make_async_copy(there, out, sem)
+    copy.start()
+    copy.wait()
 
 
 def body(layers, tile_devs, sources, green, rowcol, counts):
     shots, width = sources.shape[3], sources.shape[4]
     groups = shots // GROUP
     slots = green.shape[1]
-    meta = jnp.concatenate([rowcol.reshape(-1), counts.reshape(-1)])
-    meta = jnp.pad(meta, (0, 128 - meta.shape[0]))
-    any_space = pl.BlockSpec(memory_space=pl.ANY)
-    out = pl.pallas_call(
+    in_hbm = pl.BlockSpec(memory_space=pltpu.HBM)
+    traces = pl.pallas_call(
         functools.partial(kernel, layers, tile_devs, groups),
         out_shape=jax.ShapeDtypeStruct((2, 2, shots, width), F32),
-        in_specs=[pl.BlockSpec(memory_space=pltpu.SMEM), any_space, any_space],
-        out_specs=any_space,
+        in_specs=[in_hbm] * 4,
+        out_specs=pl.BlockSpec(memory_space=pltpu.VMEM),
         scratch_shapes=[
             pltpu.VMEM((LIVE + 2 * TILES_DEV, 2, shots, TILE), F32),
             pltpu.VMEM((SWEEPS, groups, 32, 2, GROUP, TILE), F32),
             pltpu.VMEM((SWEEPS, groups, 32, 2, GROUP, TILE), F32),
             pltpu.VMEM((32, 2, GROUP, TILE), F32),
-            pltpu.VMEM((LIVE, 4 * TILE, 2 * TILE), BF16),
+            pltpu.VMEM((LIVE, 4 * TILE, TILE), BF16),
             pltpu.VMEM((slots, 2, TILE, TILE), F32),
-            pltpu.VMEM((2 * TILES_DEV, 2, shots, TILE), F32),
-            pltpu.SMEM((128,), jnp.int32),
-            pltpu.SMEM((128,), jnp.int32),
+            pltpu.SMEM((2, slots), jnp.int32),
+            pltpu.SMEM((4,), jnp.int32),
+            pltpu.SMEM((2, slots), jnp.int32),
+            pltpu.SMEM((4,), jnp.int32),
+            pltpu.SMEM((2, slots), jnp.int32),
+            pltpu.SMEM((4,), jnp.int32),
             pltpu.SMEM((LIVE,), jnp.int32),
             pltpu.SMEM((LIVE,), jnp.int32),
             pltpu.SMEM((LIVE,), jnp.int32),
             pltpu.SMEM((LIVE, LIVE), F32),
             pltpu.SMEM((2 * TILES_DEV,), jnp.int32),
             pltpu.SMEM((32,), jnp.int32),
-            pltpu.SemaphoreType.DMA((2 * TILES_DEV + 1,)),
-            pltpu.SemaphoreType.DMA((2 * TILES_DEV,)),
-            pltpu.SemaphoreType.DMA((2,)),
-            pltpu.SemaphoreType.DMA((2,)),
+            pltpu.SemaphoreType.DMA((2 * TILES_DEV + 3,)),
+            pltpu.SemaphoreType.DMA((2, 2)),
+            pltpu.SemaphoreType.DMA((2, 2)),
             pltpu.SemaphoreType.DMA((SWEEPS, groups, 6)),
             pltpu.SemaphoreType.DMA((SWEEPS, groups, 6)),
         ],
-        compiler_params=pltpu.CompilerParams(collective_id=0, has_side_effects=True),
-    )(meta, sources[0], green[0])
+        compiler_params=pltpu.CompilerParams(collective_id=0, has_side_effects=True, vmem_limit_bytes=VMEM),
+    )(*[pltpu.with_memory_space_constraint(x, pltpu.HBM) for x in (rowcol[0].T, counts[0], sources[0], green[0])])
+    out = pl.pallas_call(
+        put_out,
+        out_shape=jax.ShapeDtypeStruct((2, 2, shots, width), F32),
+        in_specs=[pl.BlockSpec(memory_space=pltpu.VMEM)],
+        out_specs=in_hbm,
+        scratch_shapes=[pltpu.SemaphoreType.DMA],
+        compiler_params=pltpu.CompilerParams(vmem_limit_bytes=4 << 20),
+    )(traces)
     return out[None]
 
 

time: 51.9 us -> 46.1 us (0.89)
  local copies, waits for them, and re-layouts: 3.67 us -> 0 us
  Pallas kernels: 47.3 us -> 46 us
  other arithmetic: 0.73 us -> 0 us
    unnamed x2 -> x0, local copies, waits for them, and re-layouts: 3.06 us -> none
    pallas_call x1, Pallas kernels: 47.3 us -> 45 us  [body(): pl.pallas_call(functools.partial(kernel, layers, tile_devs, groups), out_...]
    pallas_call x0 -> x1, Pallas kernels: none -> 0.98 us  [body(): pl.pallas_call(put_out, out_shape=jax.ShapeDtypeStruct((2, 2, shots, widt...]
    concatenate x1 -> x0, other arithmetic: 0.73 us -> none  [body(): meta = jnp.concatenate([rowcol.reshape(-1), counts.reshape(-1)])]
where the time goes in v2:
time: 46.1 us; the launch traced here: 46 us
  Pallas kernels  46 us (100%)
    pallas_call x1, Pallas kernels, body(): pl.pallas_call(functools.partial(kernel, layers, tile_devs, groups), out_...  45 us
    pallas_call x1, Pallas kernels, body(): pl.pallas_call(put_out, out_shape=jax.ShapeDtypeStruct((2, 2, shots, widt...  0.98 us

profile of v2, /device:TPU:392, one launch (start us, length us, event | category | flops | bytes accessed | tf_op | source)
XLA Modules:
  0.0 46.0 jit_solution(2955111838173413569)
XLA Ops:
  0.0 45.0 %shard_map.46.there = f32[2,2,32,2048]{3,2,1,0:T(8,128)S(1)} custom-call(s32[2,20]{1,0:T(2,128)} %bitcast.9, s32[4]{0:T(128)} %bitcast.10, f32[2,2,32,2048]{3,2,1,0:T(8,128)} %bitcast.8, f32[20,2,128,128]{3,2,1,0:T(8,128)} %bitcast.7), custom_call_target="tpu_custom_call" | custom-call | tf_op jit(solution)/shard_map/pallas_call | solution.py:346
  45.0 1.0 %shard_map.47 = f32[2,2,32,2048]{3,2,1,0:T(8,128)} custom-call(f32[2,2,32,2048]{3,2,1,0:T(8,128)S(1)} %shard_map.46.there), custom_call_target="tpu_custom_call" | custom-call | tf_op jit(solution)/shard_map/pallas_call | solution.py:378

commit v3 on v2

--- a/solution.py
+++ b/solution.py
@@ -43,6 +43,7 @@
     out,
     state,
     recv,
+    recv_whole,
     send,
     stage,
     weights,
@@ -108,12 +109,16 @@
 
     @pl.when(layer == 0)
     def _():
+        recv_whole[0] = jnp.zeros((TILES_DEV, 2, GROUP, TILE), F32)
+
         @pl.loop(0, SWEEPS * groups)
         def _(i):
             recv[i // groups, i % groups, pl.ds(0, 16)] = jnp.zeros((16, 2, GROUP, TILE), F32)
 
     @pl.when(layer == layers - 1)
     def _():
+        recv_whole[1] = jnp.zeros((TILES_DEV, 2, GROUP, TILE), F32)
+
         @pl.loop(0, SWEEPS * groups)
         def _(i):
             recv[i // groups, i % groups, pl.ds(16, 16)] = jnp.zeros((16, 2, GROUP, TILE), F32)
@@ -186,12 +191,30 @@
 
     for copy in src_copies:
         copy.wait()
+    def first_own(direction):
+        q = 3 * direction
+        return pltpu.make_async_remote_copy(
+            state.at[pl.ds(SRC + direction * TILES_DEV, TILES_DEV), :, pl.ds(0, GROUP), :],
+            recv_whole.at[direction],
+            send_sem.at[0, 0, q],
+            recv_sem.at[0, 0, q],
+            device_id=links[q][1],
+            device_id_type=MESH,
+        )
+
     for g in range(groups):
         for q in (1, 2, 4, 5):
 
             @pl.when(links[q][0])
             def _(g=g, q=q):
                 first_halo(g, q).start()
+
+        if g == 0:
+            for direction in range(2):
+
+                @pl.when(links[3 * direction][0])
+                def _(direction=direction):
+                    first_own(direction).start()
 
     c0, c1, c2, c3 = [counts[k] for k in range(4)]
     p1, p2, p3 = c0, c0 + c1, c0 + c1 + c2
@@ -207,11 +230,13 @@
         col = rowcol[1, slot] - place * TILES_DEV
         reads_up = in1 & jnp.logical_not(in3)
         own = j - base + jnp.where(in3, c0, jnp.where(in2, c1, 0))
-        entry = jnp.where(col < 0, 8 + BAND + col, jnp.where(col >= TILES_DEV, 12 + col - TILES_DEV, own))
-        entry = entry + jnp.where(reads_up, 16, 0)
+        half = jnp.where(reads_up, 16, 0)
+        halo = jnp.where(col < 0, 8 + BAND + col, 12 + col - TILES_DEV)
+        inside = (col >= 0) & (col < TILES_DEV)
         target = row + jnp.where(in2, TILES_DEV, 0)
         slot_of[j] = slot
-        entry_of[j] = jnp.where(live, entry, 0)
+        entry_of[0, j] = jnp.where(live, half + jnp.where(inside, own, halo), 0)
+        entry_of[1, j] = jnp.where(live, half + jnp.where(inside, 32 + col, halo), 32)
         source_of[j] = SRC + jnp.where(live, target, 0)
         targets.append(jnp.where(live, target, 64 + j))
         lives.append(live)
@@ -256,7 +281,7 @@
                     send[k, g, i] = state[index_of(pack_of[i]), :, shots_of(g), :]
                 message(k, g, direction * 3).start()
 
-    @pl.loop(0, groups)
+    @pl.loop(1, groups)
     def _(g):
         pack_own(0, g, lambda tile: SRC + tile)
 
@@ -266,26 +291,36 @@
     def _(j):
         blocks = green[slot_of[j]] * jnp.where(j < total, 1.0, 0.0)
         re, im = blocks[0], blocks[1]
-        for row, part in enumerate((re, im)):
+        for column, part in enumerate((re.T, im.T)):
             high = part.astype(BF16)
-            weights[j, pl.ds(row * TILE, TILE)] = high
-            weights[j, pl.ds((2 + row) * TILE, TILE)] = (part - high.astype(F32)).astype(BF16)
+            weights[j, :, pl.ds(column * TILE, TILE)] = high
+            weights[j, :, pl.ds((2 + column) * TILE, TILE)] = (part - high.astype(F32)).astype(BF16)
+
+    for direction in range(2):
+
+        @pl.when(links[3 * direction][2])
+        def _(direction=direction):
+            first_own(direction).wait_recv()
+
+        stage[pl.ds(32 + direction * TILES_DEV, TILES_DEV)] = recv_whole[direction]
 
     def step(k, g):
+        later = (k > 0) | (g > 0)
+        whole = jnp.where(later, 0, 1)
         for q in range(6):
 
-            @pl.when(links[q][2])
+            @pl.when(links[q][2] & (later if q % 3 == 0 else True))
             def _(q=q):
                 message(k, g, q).wait_recv()
 
-        stage[...] = recv[k, g]
+        stage[pl.ds(0, 32)] = recv[k, g]
         terms = []
         for j in range(LIVE):
-            x = stage[entry_of[j]]
+            x = stage[entry_of[whole, j]]
             x = x.reshape(2 * GROUP, TILE)
             high = x.astype(BF16)
             both = jnp.concatenate([high, (x - high.astype(F32)).astype(BF16)], axis=0)
-            p = lax.dot_general(both, weights[j], (((1,), (1,)), ((), ())), preferred_element_type=F32)
+            p = lax.dot_general(both, weights[j], (((1,), (0,)), ((), ())), preferred_element_type=F32)
             p = p[:, : 2 * TILE] + p[:, 2 * TILE :]
             p = p[: 2 * GROUP] + p[2 * GROUP :]
             by_re, by_im = p[:, :TILE], p[:, TILE:]
@@ -323,11 +358,17 @@
     def _(i):
         step(i // groups, i % groups)
 
+    for direction in range(2):
+
+        @pl.when(links[3 * direction][0])
+        def _(direction=direction):
+            first_own(direction).wait_send()
+
     @pl.loop(0, SWEEPS * groups)
     def _(i):
         for q in range(6):
 
-            @pl.when(links[q][0])
+            @pl.when(links[q][0] & ((i > 0) if q % 3 == 0 else True))
             def _(q=q):
                 message(i // groups, i % groups, q).wait_send()
 
@@ -351,9 +392,10 @@
         scratch_shapes=[
             pltpu.VMEM((LIVE + 2 * TILES_DEV, 2, shots, TILE), F32),
             pltpu.VMEM((SWEEPS, groups, 32, 2, GROUP, TILE), F32),
+            pltpu.VMEM((2, TILES_DEV, 2, GROUP, TILE), F32),
             pltpu.VMEM((SWEEPS, groups, 32, 2, GROUP, TILE), F32),
-            pltpu.VMEM((32, 2, GROUP, TILE), F32),
-            pltpu.VMEM((LIVE, 4 * TILE, TILE), BF16),
+            pltpu.VMEM((64, 2, GROUP, TILE), F32),
+            pltpu.VMEM((LIVE, TILE, 4 * TILE), BF16),
             pltpu.VMEM((slots, 2, TILE, TILE), F32),
             pltpu.SMEM((2, slots), jnp.int32),
             pltpu.SMEM((4,), jnp.int32),
@@ -362,7 +404,7 @@
             pltpu.SMEM((2, slots), jnp.int32),
             pltpu.SMEM((4,), jnp.int32),
             pltpu.SMEM((LIVE,), jnp.int32),
-            pltpu.SMEM((LIVE,), jnp.int32),
+            pltpu.SMEM((2, LIVE), jnp.int32),
             pltpu.SMEM((LIVE,), jnp.int32),
             pltpu.SMEM((LIVE, LIVE), F32),
             pltpu.SMEM((2 * TILES_DEV,), jnp.int32),

time: 46.1 us -> 44.1 us (0.957)
  Pallas kernels: 46 us -> 44 us
    pallas_call x1, Pallas kernels: 45 us -> 43 us  [body(): pl.pallas_call(functools.partial(kernel, layers, tile_devs, groups), out_...]
where the time goes in v3:
time: 44.1 us; the launch traced here: 44 us
  Pallas kernels  44 us (100%)
    pallas_call x1, Pallas kernels, body(): pl.pallas_call(functools.partial(kernel, layers, tile_devs, groups), out_...  43 us
    pallas_call x1, Pallas kernels, body(): pl.pallas_call(put_out, out_shape=jax.ShapeDtypeStruct((2, 2, shots, widt...  0.98 us

profile of v3, /device:TPU:392, one launch (start us, length us, event | category | flops | bytes accessed | tf_op | source)
XLA Modules:
  0.0 44.0 jit_solution(8351214668520304973)
XLA Ops:
  0.0 43.0 %shard_map.46.there = f32[2,2,32,2048]{3,2,1,0:T(8,128)S(1)} custom-call(s32[2,20]{1,0:T(2,128)} %bitcast.9, s32[4]{0:T(128)} %bitcast.10, f32[2,2,32,2048]{3,2,1,0:T(8,128)} %bitcast.8, f32[20,2,128,128]{3,2,1,0:T(8,128)} %bitcast.7), custom_call_target="tpu_custom_call" | custom-call | tf_op jit(solution)/shard_map/pallas_call | solution.py:387
  43.0 1.0 %shard_map.47 = f32[2,2,32,2048]{3,2,1,0:T(8,128)} custom-call(f32[2,2,32,2048]{3,2,1,0:T(8,128)S(1)} %shard_map.46.there), custom_call_target="tpu_custom_call" | custom-call | tf_op jit(solution)/shard_map/pallas_call | solution.py:420

commit v4 on v3

--- a/solution.py
+++ b/solution.py
@@ -302,11 +302,21 @@
         def _(direction=direction):
             first_own(direction).wait_recv()
 
+        @pl.when(links[3 * direction][0])
+        def _(direction=direction):
+            first_own(direction).wait_send()
+
         stage[pl.ds(32 + direction * TILES_DEV, TILES_DEV)] = recv_whole[direction]
 
     def step(k, g):
         later = (k > 0) | (g > 0)
         whole = jnp.where(later, 0, 1)
+        for q in range(6):
+
+            @pl.when(links[q][0] & (later if q % 3 == 0 else True))
+            def _(q=q):
+                message(k, g, q).wait_send()
+
         for q in range(6):
 
             @pl.when(links[q][2] & (later if q % 3 == 0 else True))
@@ -335,18 +345,24 @@
 
         @pl.when(k < SWEEPS - 1)
         def _():
-            for q in (1, 2, 4, 5):
-                direction, kind = q // 3, q % 3
-
-                @pl.when(links[q][0])
-                def _(q=q, direction=direction, kind=kind):
-                    first = 0 if kind == 1 else TILES_DEV - BAND
-                    for e in range(BAND):
-                        found = where_is[direction * TILES_DEV + first + e]
-                        send[k + 1, g, direction * 16 + 4 + 4 * kind + e] = state[found, :, shots_of(g), :]
-                    message(k + 1, g, q).start()
-
-            pack_own(k + 1, g, lambda tile: where_is[tile])
+            for direction, own_ok in ((0, down_ok), (1, up_ok)):
+                for kind in (1, 2):
+                    q = 3 * direction + kind
+
+                    @pl.when(links[q][0])
+                    def _(q=q, direction=direction, kind=kind):
+                        first = 0 if kind == 1 else TILES_DEV - BAND
+                        for e in range(BAND):
+                            found = where_is[direction * TILES_DEV + first + e]
+                            send[k + 1, g, direction * 16 + 4 + 4 * kind + e] = state[found, :, shots_of(g), :]
+                        message(k + 1, g, q).start()
+
+                @pl.when(own_ok)
+                def _(direction=direction):
+                    for e in range(OWN[direction]):
+                        i = direction * 16 + e
+                        send[k + 1, g, i] = state[where_is[pack_of[i]], :, shots_of(g), :]
+                    message(k + 1, g, direction * 3).start()
 
         @pl.when(k == SWEEPS - 1)
         def _():
@@ -357,26 +373,6 @@
     @pl.loop(0, SWEEPS * groups)
     def _(i):
         step(i // groups, i % groups)
-
-    for direction in range(2):
-
-        @pl.when(links[3 * direction][0])
-        def _(direction=direction):
-            first_own(direction).wait_send()
-
-    @pl.loop(0, SWEEPS * groups)
-    def _(i):
-        for q in range(6):
-
-            @pl.when(links[q][0] & ((i > 0) if q % 3 == 0 else True))
-            def _(q=q):
-                message(i // groups, i % groups, q).wait_send()
-
-
-def put_out(there, out, sem):
-    copy = pltpu.make_async_copy(there, out, sem)
-    copy.start()
-    copy.wait()
 
 
 def body(layers, tile_devs, sources, green, rowcol, counts):
@@ -417,15 +413,7 @@
         ],
         compiler_params=pltpu.CompilerParams(collective_id=0, has_side_effects=True, vmem_limit_bytes=VMEM),
     )(*[pltpu.with_memory_space_constraint(x, pltpu.HBM) for x in (rowcol[0].T, counts[0], sources[0], green[0])])
-    out = pl.pallas_call(
-        put_out,
-        out_shape=jax.ShapeDtypeStruct((2, 2, shots, width), F32),
-        in_specs=[pl.BlockSpec(memory_space=pltpu.VMEM)],
-        out_specs=in_hbm,
-        scratch_shapes=[pltpu.SemaphoreType.DMA],
-        compiler_params=pltpu.CompilerParams(vmem_limit_bytes=4 << 20),
-    )(traces)
-    return out[None]
+    return traces[None]
 
 
 def solution(mesh):

time: 44.1 us -> 43.5 us (0.986)
  Pallas kernels: 44 us -> 42.4 us
  local copies, waits for them, and re-layouts: 0 us -> 0.97 us
    pallas_call x1 -> x0, Pallas kernels: 0.98 us -> none  [body(): pl.pallas_call(put_out, out_shape=jax.ShapeDtypeStruct((2, 2, shots, widt...]
    unnamed x0 -> x1, local copies, waits for them, and re-layouts: none -> 0.97 us
    pallas_call x1, Pallas kernels: 43 us -> 42.4 us  [body(): pl.pallas_call(functools.partial(kernel, layers, tile_devs, groups), out_...]
where the time goes in v4:
time: 43.5 us; the launch traced here: 43.4 us
  Pallas kernels  42.4 us (97%)
  local copies, waits for them, and re-layouts  0.97 us (2%)
    pallas_call x1, Pallas kernels, body(): pl.pallas_call(functools.partial(kernel, layers, tile_devs, groups), out_...  42.4 us
    unnamed x1, local copies, waits for them, and re-layouts  0.97 us

profile of v4, /device:TPU:392, one launch (start us, length us, event | category | flops | bytes accessed | tf_op | source)
XLA Modules:
  0.0 43.4 jit_solution(1564528069873564949)
XLA Ops:
  0.0 42.4 %shard_map.46 = f32[2,2,32,2048]{3,2,1,0:T(8,128)S(1)} custom-call(s32[2,20]{1,0:T(2,128)} %bitcast.10, s32[4]{0:T(128)} %bitcast.11, f32[2,2,32,2048]{3,2,1,0:T(8,128)} %bitcast.9, f32[20,2,128,128]{3,2,1,0:T(8,128)} %bitcast.8), custom_call_target="tpu_custom_call" | custom-call | tf_op jit(solution)/shard_map/pallas_call | solution.py:383
  42.4 1.0 %copy.6 = f32[1,2,2,32,2048]{4,3,2,1,0:T(8,128)} copy(f32[1,2,2,32,2048]{4,3,2,1,0:T(8,128)S(1)} %bitcast.7) | data formatting | bytes 2097152

commit v5 on v4

--- a/solution.py
+++ b/solution.py
@@ -70,6 +70,7 @@
     place = lax.axis_index("tile")
     up_ok, down_ok = layer > 0, layer < layers - 1
     low_ok, high_ok = place > 0, place < tile_devs - 1
+    even = layer % 2 == 0
 
     lower, upper = layer + 1, layer - 1
     links = [
@@ -345,11 +346,11 @@
 
         @pl.when(k < SWEEPS - 1)
         def _():
-            for direction, own_ok in ((0, down_ok), (1, up_ok)):
+            for direction, turn in ((1, even), (0, True), (1, jnp.logical_not(even))):
                 for kind in (1, 2):
                     q = 3 * direction + kind
 
-                    @pl.when(links[q][0])
+                    @pl.when(links[q][0] & turn)
                     def _(q=q, direction=direction, kind=kind):
                         first = 0 if kind == 1 else TILES_DEV - BAND
                         for e in range(BAND):
@@ -357,7 +358,7 @@
                             send[k + 1, g, direction * 16 + 4 + 4 * kind + e] = state[found, :, shots_of(g), :]
                         message(k + 1, g, q).start()
 
-                @pl.when(own_ok)
+                @pl.when(links[3 * direction][0] & turn)
                 def _(direction=direction):
                     for e in range(OWN[direction]):
                         i = direction * 16 + e

time: 43.5 us -> 43.6 us (level)
  no operation moved by 1% of the time
where the time goes in v5:
time: 43.6 us; the launch traced here: 43.4 us
  Pallas kernels  42.4 us (97%)
  local copies, waits for them, and re-layouts  0.97 us (2%)
    pallas_call x1, Pallas kernels, body(): pl.pallas_call(functools.partial(kernel, layers, tile_devs, groups), out_...  42.4 us
    unnamed x1, local copies, waits for them, and re-layouts  0.97 us

profile of v5, /device:TPU:392, one launch (start us, length us, event | category | flops | bytes accessed | tf_op | source)
XLA Modules:
  0.0 43.4 jit_solution(2054574792836182265)
XLA Ops:
  0.0 42.4 %shard_map.46 = f32[2,2,32,2048]{3,2,1,0:T(8,128)S(1)} custom-call(s32[2,20]{1,0:T(2,128)} %bitcast.10, s32[4]{0:T(128)} %bitcast.11, f32[2,2,32,2048]{3,2,1,0:T(8,128)} %bitcast.9, f32[20,2,128,128]{3,2,1,0:T(8,128)} %bitcast.8), custom_call_target="tpu_custom_call" | custom-call | tf_op jit(solution)/shard_map/pallas_call | solution.py:384
  42.5 1.0 %copy.6 = f32[1,2,2,32,2048]{4,3,2,1,0:T(8,128)} copy(f32[1,2,2,32,2048]{4,3,2,1,0:T(8,128)S(1)} %bitcast.7) | data formatting | bytes 2097152
